TPU v7x, 256 devices: a whole 4x4x8 slice. The times are simulated.
256 devices in a mesh: dp: 64 (over z, y, core), section: 4 (over x).
Axes of the slice: x: 4, y: 4, z: 8, core: 2. Of those that a mesh axis runs over, the one named last changes fastest.
Arguments:
- query_hidden: bfloat16 [32768, 4096], P('dp', 'section'), may hold values from -0.5 to 0.5
- tool_hidden: bfloat16 [32768, 4096], P('dp', 'section'), may hold values from -0.5 to 0.5
- norm_gain: float32 [4096], P('section'), may hold values from 0.5 to 1.5
- positive_tool: int32 [32768], P('dp'), may hold values from 0 to 511
- hard_owner: int32 [32768, 2], P('dp'), may hold values from 0 to 63, as said below
- hard_row: int32 [32768, 2], P('dp'), may hold values from 0 to 511
- hard_valid: int32 [32768, 2], P('dp'), may hold values from 0 to 1
Outputs:
- query_grad: bfloat16 [32768, 4096], P('dp', 'section')
- tool_grad: bfloat16 [32768, 4096], P('dp', 'section')
- gain_grad: float32 [4096], P('section')
Inputs may be any that keep to these rules, and one draw needn't show every extreme that they name: `hard_owner`: each dp index's valid slots name any one owner at most 32 times; two owners, the same for every dp index and drawn from the seed, are named exactly 32 times by the valid slots of every dp index.
All inputs are finite; a program needn't handle non-finite values.
Results may differ from a plain program's by a relative error of at most 0.0067.
Values may be sent and summed in bfloat16 or wider, within the bound.
A program may use at most 128 MiB of HBM per device.

v0:
```python
import jax
import jax.numpy as jnp
from jax import lax
from jax.sharding import PartitionSpec as P

EPSILON = 1e-06
SOFTMAX_TEMP = 0.05


def softmax_grads(shard_scores, negative_scores, positive, valid_mask):
    selected_rows = lax.broadcasted_iota(jnp.int32, shard_scores.shape, 1) == positive[:, None]
    softmax_weights = jnp.exp(shard_scores / SOFTMAX_TEMP)
    shard_probabilities = softmax_weights / jnp.sum(softmax_weights, axis=1, keepdims=True)
    positive_score = jnp.sum(jnp.where(selected_rows, shard_scores, 0.0), axis=1)
    positive_weight = jnp.exp(positive_score / SOFTMAX_TEMP)
    negative_weights = jnp.where(valid_mask > 0, jnp.exp(negative_scores / SOFTMAX_TEMP), 0.0)
    negative_weight_sum = positive_weight + jnp.sum(negative_weights, axis=1)
    shard_gradients = (
        (
            shard_probabilities
            + jnp.where(selected_rows, (positive_weight / negative_weight_sum - 2.0)[:, None], 0.0)
        )
        / SOFTMAX_TEMP
    ).astype(jnp.bfloat16)
    negative_gradients = (negative_weights / (negative_weight_sum[:, None] * SOFTMAX_TEMP)).astype(
        jnp.bfloat16
    )
    return (shard_gradients, negative_gradients)


def body(query_hidden, tool_hidden, norm_gain, positive_tool, hard_owner, hard_row, hard_valid):
    query_count, features = query_hidden.shape
    per_query = hard_owner.shape[1]
    group_size = lax.axis_size("dp")
    capacity = max(2, 2 * query_count * per_query // group_size)
    query_scaled = query_hidden.astype(jnp.float32) * norm_gain
    tool_scaled = tool_hidden.astype(jnp.float32) * norm_gain
    query_squares, tool_squares = lax.psum(
        (jnp.sum(query_scaled * query_scaled, axis=1), jnp.sum(tool_scaled * tool_scaled, axis=1)),
        "section",
    )
    query_norm = jnp.sqrt(query_squares + EPSILON)
    tool_norm = jnp.sqrt(tool_squares + EPSILON)
    query_unit32 = query_scaled / query_norm[:, None]
    tool_unit32 = tool_scaled / tool_norm[:, None]
    query_unit = query_unit32.astype(jnp.bfloat16)
    tool_unit = tool_unit32.astype(jnp.bfloat16)
    owners = hard_owner.reshape(-1)
    wanted_rows = hard_row.reshape(-1)
    usable = hard_valid.reshape(-1) > 0
    owner_table = (
        (owners[:, None] == jnp.arange(group_size, dtype=jnp.int32)[None, :]) & usable[:, None]
    ).astype(jnp.int32)
    earlier = jnp.cumsum(owner_table, axis=0) - owner_table
    slot_place = jnp.sum(earlier * owner_table, axis=1)
    target = jnp.where(usable, owners * capacity + slot_place, group_size * capacity)
    requests = (
        jnp.zeros((group_size * capacity,), jnp.int32)
        .at[target]
        .set(wanted_rows, mode="drop")
        .reshape(group_size, capacity)
    )
    indices = lax.all_to_all(requests, "dp", split_axis=0, concat_axis=0, tiled=True)
    answers = tool_unit[indices]
    back = lax.all_to_all(answers, "dp", split_axis=0, concat_axis=0, tiled=True)
    lookup = jnp.where(usable, target, 0)
    hard_units = back.reshape(group_size * capacity, features)[lookup].reshape(
        query_count, per_query, features
    )
    local_part = lax.dot_general(
        query_unit, tool_unit, (((1,), (1,)), ((), ())), preferred_element_type=jnp.float32
    )
    hard_part = jnp.einsum("qd,qkd->qk", query_unit, hard_units, preferred_element_type=jnp.float32)
    shard_scores, negative_scores = (
        lax.psum(local_part.astype(jnp.bfloat16), "section").astype(jnp.float32),
        lax.psum(hard_part.astype(jnp.bfloat16), "section").astype(jnp.float32),
    )
    shard_gradients, negative_gradients = softmax_grads(
        shard_scores, negative_scores, positive_tool, hard_valid
    )
    query_pull = jnp.dot(shard_gradients, tool_unit, preferred_element_type=jnp.float32)
    query_pull = query_pull + jnp.einsum(
        "qk,qkd->qd", negative_gradients, hard_units, preferred_element_type=jnp.float32
    )
    tool_pull = lax.dot_general(
        shard_gradients, query_unit, (((0,), (0,)), ((), ())), preferred_element_type=jnp.float32
    )
    slot_queries = jnp.repeat(query_unit, per_query, axis=0)
    returned = negative_gradients.reshape(-1)[:, None].astype(jnp.float32) * slot_queries.astype(
        jnp.float32
    )
    outgoing = (
        jnp.zeros((group_size * capacity, features), jnp.float32)
        .at[target]
        .set(returned, mode="drop")
    )
    arrived = lax.all_to_all(
        outgoing.reshape(group_size, capacity, features).astype(jnp.bfloat16),
        "dp",
        split_axis=0,
        concat_axis=0,
        tiled=True,
    ).astype(jnp.float32)
    tool_pull = tool_pull.at[indices.reshape(-1)].add(arrived.reshape(-1, features))
    query_inner, tool_inner = lax.psum(
        (jnp.sum(query_unit32 * query_pull, axis=1), jnp.sum(tool_unit32 * tool_pull, axis=1)),
        "section",
    )
    query_back = (query_pull - query_unit32 * query_inner[:, None]) / query_norm[:, None]
    tool_back = (tool_pull - tool_unit32 * tool_inner[:, None]) / tool_norm[:, None]
    query_grad = (query_back * norm_gain).astype(jnp.bfloat16)
    tool_grad = (tool_back * norm_gain).astype(jnp.bfloat16)
    gain_terms = jnp.sum(query_back * query_hidden.astype(jnp.float32), axis=0) + jnp.sum(
        tool_back * tool_hidden.astype(jnp.float32), axis=0
    )
    gain_grad = lax.psum(gain_terms, "dp")
    return (query_grad, tool_grad, gain_grad)


def solution(mesh):
    return jax.shard_map(
        body,
        mesh=mesh,
        in_specs=(
            P("dp", "section"),
            P("dp", "section"),
            P("section"),
            P("dp"),
            P("dp", None),
            P("dp", None),
            P("dp", None),
        ),
        out_specs=(P("dp", "section"), P("dp", "section"), P("section")),
        check_vma=False,
    )
```

profile of v0, /device:TPU:1, one launch (start us, length us, event | category | flops | bytes accessed | tf_op | source)
XLA Modules:
  0.0 498.0 jit_solution(5765499487373668806)
XLA Ops:
  7.2 0.7 broadcast_compare_fusion
  7.9 0.2 copy.20
  8.1 0.2 gt.35
  8.3 0.2 gt.34
  8.4 0.8 copy.22
  9.3 0.0 copy-start
  9.3 0.0 copy-start.1
  9.3 0.0 copy-start.4
  9.3 0.2 eq.39
  9.5 0.2 eq.35
  9.7 0.2 gt.33
  9.8 0.8 broadcast_multiply_fusion
  10.7 18.0 %reduce-window.6 = s32[64,8,128]{2,1,0:T(8,128)S(1)} reduce-window(s32[64,8,128]{2,1,0:T(8,128)S(1)} %fusion.28, s32[]{:T(128)} %constant.12.clone.1), window={size=1x1x128 pad=0_0x0_0x127_0}, to_apply=%region_7.8 | reduce-window | flops 8323072 | bytes 524292 | tf_op jit(solution)/shard_map/reduce-window
  28.7 0.1 slice.12
  28.8 0.1 copy.26
  29.0 0.1 copy.27
  29.1 0.1 broadcast_add_fusion
  29.2 0.1 copy.21
  29.4 0.2 mul.109
  29.6 0.1 copy.28
  29.7 0.2 reshape.249
  29.9 0.1 fusion.25
  30.0 4.3 scatter_custom_fusion
  34.3 0.7 all_to_all.14
  35.0 13.1 %all-to-all-start = ((s32[64,1,32]{2,1,0:T(1,128)}), s32[64,1,32]{2,1,0:T(1,128)S(1)}, u32[]{:S(2)}, u32[]{:S(2)}) async-start(s32[64,1,32]{2,1,0:T(1,128)} %bitcast.5), calls=%async_computation | async-start | bytes 65536 | tf_op jit(solution)/shard_map/all_to_all | solution.py:63
  48.2 0.6 fusion.10
  48.8 9.0 %all-reduce.1 = (f32[512]{0:T(512)S(1)}, f32[512]{0:T(512)S(1)}) all-reduce(f32[512]{0:T(512)S(1)} %get-tuple-element.8, f32[512]{0:T(512)S(1)} %get-tuple-element.7), channel_id=1, replica_groups=mesh['dp'=64,'section'=4] {'section'}, use_global_device_ids=true, to_apply=%region_3.0 | all-reduce | flops 1024 | bytes 8192 | tf_op jit(solution)/shard_map/psum | solution.py:38
  57.8 1.8 fusion.33
  59.6 0.0 all-to-all-done
  59.6 0.1 reshape.231
  59.7 9.7 %gather_fusion = bf16[2048,1024]{1,0:T(8,128)(2,1)} fusion(bf16[512,1024]{1,0:T(8,128)(2,1)S(1)} %get-tuple-element.23, s32[2048]{0:T(1024)S(1)} %broadcast_clamp_fusion), kind=kCustom, calls=%fused_computation | custom fusion | bytes 8396800 | tf_op jit(solution)/shard_map/gather | solution.py:64
  69.4 12.0 %all-to-all-start.1 = ((bf16[64,32,1024]{2,1,0:T(8,128)(2,1)}), bf16[64,32,1024]{2,1,0:T(8,128)(2,1)}, u32[]{:S(2)}, u32[]{:S(2)}) async-start(bf16[64,32,1024]{2,1,0:T(8,128)(2,1)} %bitcast.46), calls=%async_computation.1 | async-start | bytes 8388608 | tf_op jit(solution)/shard_map/all_to_all | solution.py:65
  81.4 0.2 all-reduce.4.cloned.1.call-start
  81.6 2.8 convolution_convert_fusion
  84.4 0.0 all-reduce.4.cloned.1.call-update
  84.4 4.3 broadcast_in_dim.32
  88.7 6.0 %convert_element_type.86 = f32[1024,1024]{1,0:T(8,128)} reshape(f32[512,2,1024]{2,1,0:T(2,128)} %broadcast_in_dim.32) | data formatting | bytes 8388608 | tf_op jit(solution)/shard_map/convert_element_type | solution.py:89
  94.7 35.9 %all-reduce.4.cloned.1.call-done = bf16[512,512]{1,0:T(8,128)(2,1)} async-done(((bf16[512,512]{1,0:T(8,128)(2,1)}), bf16[512,512]{1,0:T(8,128)(2,1)}) %all-reduce.4.cloned.1.call-update) | async-done | bytes 524304 | tf_op jit(solution)/shard_map/psum | solution.py:75
  130.7 1.5 fusion.18
  132.2 43.9 %all-to-all-done.1 = bf16[64,32,1024]{2,1,0:T(8,128)(2,1)} async-done(((bf16[64,32,1024]{2,1,0:T(8,128)(2,1)}), bf16[64,32,1024]{2,1,0:T(8,128)(2,1)}, u32[]{:S(2)}, u32[]{:S(2)}) %all-to-all-start.1) | async-done | bytes 4194336 | tf_op jit(solution)/shard_map/all_to_all | solution.py:65
  176.1 8.8 %gather_fusion.1 = bf16[1024,1024]{1,0:T(8,128)(2,1)} fusion(bf16[2048,1024]{1,0:T(8,128)(2,1)} %bitcast.8, s32[1024]{0:T(1024)S(1)} %broadcast_clamp_fusion.1), kind=kCustom, calls=%fused_computation.1 | custom fusion | bytes 4198400 | tf_op jit(solution)/shard_map/gather | solution.py:67
  184.9 4.1 reshape.222
  189.0 6.3 %fusion.14 = bf16[512,1,2]{2,1,0:T(2,128)(2,1)S(1)} fusion(bf16[512,2,1024]{2,1,0:T(2,128)(2,1)} %reshape.222, bf16[512,1024,1]{1,0,2:T(8,128)(2,1)} %bitcast.47), kind=kOutput, calls=%fused_computation.30 | convolution fusion | flops 2097152 | bytes 3147776 | tf_op jit(solution)/shard_map/qd,qkd->qk/dot_general | solution.py:73
  195.3 0.1 copy.32
  195.5 6.0 %psum.52 = bf16[512,2]{0,1:T(2,128)(2,1)S(1)} all-reduce(bf16[512,2]{0,1:T(2,128)(2,1)S(1)} %bitcast.54), channel_id=1, replica_groups=mesh['dp'=64,'section'=4] {'section'}, use_global_device_ids=true, to_apply=%region_11.12 | all-reduce | flops 1024 | bytes 4096 | tf_op jit(solution)/shard_map/psum | solution.py:76
  201.5 0.2 copy.30
  201.7 0.2 reshape.226
  201.9 10.1 %scatter_custom_fusion.1 = f32[2048,1024]{1,0:T(8,128)} fusion(s32[1024]{0:T(1024)S(1)} %bitcast.57, f32[1024,1024]{1,0:T(8,128)} %convert_element_type.86, f32[]{:T(128)} %constant.9.clone.1, f32[1024]{0:T(1024)S(1)} %reshape.226), kind=kCustom, calls=%fused_computation.7 | custom fusion | flops 1048576 | bytes 12587012 | tf_op jit(solution)/shard_map/scatter | solution.py:95
  212.0 6.0 %convert_element_type.87 = bf16[2048,1024]{1,0:T(8,128)(2,1)} convert(f32[2048,1024]{1,0:T(8,128)} %scatter_custom_fusion.1) | non-fusion elementwise | flops 2097152 | bytes 12582912 | tf_op jit(solution)/shard_map/convert_element_type | solution.py:98
  218.0 8.8 %all-to-all-start.2 = ((bf16[64,32,1024]{2,1,0:T(8,128)(2,1)}), bf16[64,32,1024]{2,1,0:T(8,128)(2,1)}, u32[]{:S(2)}, u32[]{:S(2)}) async-start(bf16[64,32,1024]{2,1,0:T(8,128)(2,1)} %bitcast.45), calls=%async_computation.2 | async-start | bytes 8388608 | tf_op jit(solution)/shard_map/all_to_all | solution.py:97
  226.8 0.5 broadcast.204
  227.4 0.7 reduce.3
  228.1 0.1 reshape.223
  228.2 0.2 copy.33
  228.4 3.8 fusion.34
  232.2 3.7 fusion.37
  235.9 85.9 %all-to-all-done.2 = bf16[64,32,1024]{2,1,0:T(8,128)(2,1)} async-done(((bf16[64,32,1024]{2,1,0:T(8,128)(2,1)}), bf16[64,32,1024]{2,1,0:T(8,128)(2,1)}, u32[]{:S(2)}, u32[]{:S(2)}) %all-to-all-start.2) | async-done | bytes 4194336 | tf_op jit(solution)/shard_map/all_to_all | solution.py:97
  321.7 21.0 %scatter_custom_fusion.2 = f32[512,1024]{1,0:T(8,128)} fusion(f32[512,1024]{1,0:T(8,128)} %fusion.34, s32[2048]{0:T(1024)S(1)} %bitcast.55, bf16[2048,1024]{1,0:T(8,128)(2,1)} %bitcast.16), kind=kCustom, calls=%fused_computation.5 | custom fusion | flops 4194304 | bytes 6291456 | tf_op jit(solution)/shard_map/scatter-add | solution.py:104
  342.7 5.2 %multiply_reduce_fusion = (f32[512]{0:T(512)S(1)}, f32[512]{0:T(512)S(1)}, f32[512,1024]{1,0:T(8,128)}) fusion(f32[512,1024]{1,0:T(8,128)} %scatter_custom_fusion.2, f32[512]{0:T(512)S(1)} %get-tuple-element.25, f32[1024]{0:T(1024)S(1)} %copy-done.4, bf16[512,1024]{1,0:T(8,128)(2,1)S(1)} %copy-done.1, f32[512]{0:T(512)S(1)} %get-tuple-element.26, ...), kind=kOutput, calls=%fused_computation.25 | convolution fusion | flops 544734208 | bytes 9979904 | tf_op jit(solution)/shard_map/dot_general | solution.py:81
  347.9 7.7 %all-reduce = (f32[512]{0:T(512)S(1)}, f32[512]{0:T(512)S(1)}) all-reduce(f32[512]{0:T(512)S(1)} %get-tuple-element.6, f32[512]{0:T(512)S(1)} %get-tuple-element.5), channel_id=1, replica_groups=mesh['dp'=64,'section'=4] {'section'}, use_global_device_ids=true, to_apply=%region_14.15 | all-reduce | flops 1024 | bytes 8192 | tf_op jit(solution)/shard_map/psum | solution.py:105
  355.6 2.4 fusion.12
  358.0 2.3 fusion.11
  360.4 128.0 %psum.55 = f32[1024]{0:T(1024)} all-reduce(f32[1024]{0:T(1024)S(1)} %add.119), channel_id=1, replica_groups=mesh['dp'=64,'section'=4] {'dp'}, use_global_device_ids=true, to_apply=%region_21.22 | all-reduce | flops 1024 | bytes 8192 | tf_op jit(solution)/shard_map/psum | solution.py:116
  488.3 2.8 multiply_convert_fusion.1
  (26 shorter events, 0.2 us)
Async XLA Ops:
  7.2 22.4 %copy-start.6 = (s32[512,2]{0,1:T(2,128)S(1)}, s32[512,2]{0,1:T(2,128)}, u32[]{:S(2)}) copy-start(s32[512,2]{0,1:T(2,128)} %param.12) | copy-start | bytes 12292
  9.3 38.9 %copy-start = (bf16[512,1024]{1,0:T(8,128)(2,1)S(1)}, bf16[512,1024]{1,0:T(8,128)(2,1)}, u32[]{:S(2)}) copy-start(bf16[512,1024]{1,0:T(8,128)(2,1)} %param.7) | copy-start | bytes 3145732
  9.3 38.9 %copy-start.1 = (bf16[512,1024]{1,0:T(8,128)(2,1)S(1)}, bf16[512,1024]{1,0:T(8,128)(2,1)}, u32[]{:S(2)}) copy-start(bf16[512,1024]{1,0:T(8,128)(2,1)} %param.8) | copy-start | bytes 3145732
  9.3 38.9 %copy-start.4 = (f32[1024]{0:T(1024)S(1)}, f32[1024]{0:T(1024)}, u32[]{:S(2)}) copy-start(f32[1024]{0:T(1024)} %param.9) | copy-start | bytes 12292
  35.0 24.6 %all-to-all-start = ((s32[64,1,32]{2,1,0:T(1,128)}), s32[64,1,32]{2,1,0:T(1,128)S(1)}, u32[]{:S(2)}, u32[]{:S(2)}) async-start(s32[64,1,32]{2,1,0:T(1,128)} %bitcast.5), calls=%async_computation | async-start | bytes 65536 | tf_op jit(solution)/shard_map/all_to_all | solution.py:63
  69.4 106.7 %all-to-all-start.1 = ((bf16[64,32,1024]{2,1,0:T(8,128)(2,1)}), bf16[64,32,1024]{2,1,0:T(8,128)(2,1)}, u32[]{:S(2)}, u32[]{:S(2)}) async-start(bf16[64,32,1024]{2,1,0:T(8,128)(2,1)} %bitcast.46), calls=%async_computation.1 | async-start | bytes 8388608 | tf_op jit(solution)/shard_map/all_to_all | solution.py:65
  81.4 49.3 %all-reduce.4.cloned.1.call-start = ((), (), s32[]{:S(2)}) async-start(), calls=%async_computation.3 | async-start | bytes 1048576 | tf_op jit(solution)/shard_map/psum | solution.py:75
  88.7 42.0 %copy-start.7 = (s32[512]{0:T(512)S(1)}, s32[512]{0:T(512)}, u32[]{:S(2)}) copy-start(s32[512]{0:T(512)} %param.10) | copy-start | bytes 6148
  189.0 12.5 %copy-start.5 = (s32[512,2]{0,1:T(2,128)S(1)}, s32[512,2]{0,1:T(2,128)}, u32[]{:S(2)}) copy-start(s32[512,2]{0,1:T(2,128)} %param.13) | copy-start | bytes 12292
  218.0 103.7 %all-to-all-start.2 = ((bf16[64,32,1024]{2,1,0:T(8,128)(2,1)}), bf16[64,32,1024]{2,1,0:T(8,128)(2,1)}, u32[]{:S(2)}, u32[]{:S(2)}) async-start(bf16[64,32,1024]{2,1,0:T(8,128)(2,1)} %bitcast.45), calls=%async_computation.2 | async-start | bytes 8388608 | tf_op jit(solution)/shard_map/all_to_all | solution.py:97
  228.4 3.8 copy-start.3
  355.6 2.4 copy-start.2
Sparse Core Ops, SparseCore 0:
  85.1 45.5 all-reduce.3
where the time goes:
time: 499 us; the launch traced here: 498 us
  waiting for transfers between devices  166 us (33%)
  blocking collectives  151 us (30%)
  other arithmetic  69.2 us (14%)
  local copies, waits for them, and re-layouts  42.2 us (8%)
  starting transfers between devices  34.2 us (7%)
  matrix products  21.8 us (4%)
  between operations  14.3 us (3%)
    psum x1, blocking collectives, body(): gain_grad = lax.psum(gain_terms, 'dp')  128 us
    all_to_all x1, waiting for transfers between devices, body(): lax.all_to_all(outgoing.reshape(group_size, capacity, features).astype(jn...  85.9 us
    all_to_all x1, waiting for transfers between devices, body(): lax.all_to_all(answers, 'dp', split_axis=0, concat_axis=0, tiled=True)  43.9 us
    psum x1, waiting for transfers between devices, body(): lax.psum(local_part.astype(jnp.bfloat16), 'section').astype(jnp.float32)  35.9 us
    scatter-add x1, other arithmetic, body(): tool_pull.at[indices.reshape(-1)].add(arrived.reshape(-1, features))  21 us
    another operation x3, other arithmetic  18.2 us
    all_to_all x1, starting transfers between devices, body(): lax.all_to_all(requests, 'dp', split_axis=0, concat_axis=0, tiled=True)  13.1 us
    all_to_all x1, starting transfers between devices, body(): lax.all_to_all(answers, 'dp', split_axis=0, concat_axis=0, tiled=True)  12 us
  transfers between devices with their start and end apart: 4, of which 3 were waited for; matrix products, arithmetic and copies ran while one was open for 5% of the time, Pallas kernels for 0%

commit v1 on v0

--- a/solution.py
+++ b/solution.py
@@ -113,7 +113,7 @@
     gain_terms = jnp.sum(query_back * query_hidden.astype(jnp.float32), axis=0) + jnp.sum(
         tool_back * tool_hidden.astype(jnp.float32), axis=0
     )
-    gain_grad = lax.psum(gain_terms, "dp")
+    gain_grad = jnp.sum(lax.all_gather(gain_terms, "dp"), axis=0)
     return (query_grad, tool_grad, gain_grad)
 
 

time: 499 us -> 419 us (0.84)
  blocking collectives: 151 us -> 70 us
    psum x1 -> x0, blocking collectives: 128 us -> none  [body(): gain_grad = lax.psum(gain_terms, 'dp')]
    all_gather x0 -> x1, blocking collectives: none -> 47.4 us  [body(): gain_grad = jnp.sum(lax.all_gather(gain_terms, 'dp'), axis=0)]
  transfers between devices with their start and end apart: 4 -> 4, of which waited for: 3 -> 3; matrix products, arithmetic and copies ran while one was open for 5% -> 6% of each run, Pallas kernels for 0% -> 0%
where the time goes in v1:
time: 419 us; the launch traced here: 418 us
  waiting for transfers between devices  166 us (40%)
  blocking collectives  70 us (17%)
  other arithmetic  69.8 us (17%)
  local copies, waits for them, and re-layouts  42.2 us (10%)
  starting transfers between devices  34.2 us (8%)
  matrix products  21.8 us (5%)
  between operations  14.3 us (3%)
    all_to_all x1, waiting for transfers between devices, body(): lax.all_to_all(outgoing.reshape(group_size, capacity, features).astype(jn...  85.9 us
    all_gather x1, blocking collectives, body(): gain_grad = jnp.sum(lax.all_gather(gain_terms, 'dp'), axis=0)  47.4 us
    all_to_all x1, waiting for transfers between devices, body(): lax.all_to_all(answers, 'dp', split_axis=0, concat_axis=0, tiled=True)  43.9 us
    psum x1, waiting for transfers between devices, body(): lax.psum(local_part.astype(jnp.bfloat16), 'section').astype(jnp.float32)  35.9 us
    scatter-add x1, other arithmetic, body(): tool_pull.at[indices.reshape(-1)].add(arrived.reshape(-1, features))  21 us
    another operation x3, other arithmetic  18.2 us
    all_to_all x1, starting transfers between devices, body(): lax.all_to_all(requests, 'dp', split_axis=0, concat_axis=0, tiled=True)  13.1 us
    all_to_all x1, starting transfers between devices, body(): lax.all_to_all(answers, 'dp', split_axis=0, concat_axis=0, tiled=True)  12 us
  transfers between devices with their start and end apart: 4, of which 3 were waited for; matrix products, arithmetic and copies ran while one was open for 6% of the time, Pallas kernels for 0%

profile of v1, /device:TPU:1, one launch (start us, length us, event | category | flops | bytes accessed | tf_op | source)
XLA Modules:
  0.0 418.0 jit_solution(11943338515779134029)
XLA Ops:
  7.2 0.7 broadcast_compare_fusion
  7.9 0.2 copy.31
  8.1 0.2 gt.35
  8.3 0.2 gt.34
  8.4 0.8 copy.33
  9.3 0.0 copy-start
  9.3 0.0 copy-start.1
  9.3 0.0 copy-start.4
  9.3 0.2 eq.39
  9.5 0.2 eq.35
  9.7 0.2 gt.33
  9.8 0.8 broadcast_multiply_fusion
  10.7 18.0 %reduce-window.6 = s32[64,8,128]{2,1,0:T(8,128)S(1)} reduce-window(s32[64,8,128]{2,1,0:T(8,128)S(1)} %fusion.28, s32[]{:T(128)} %constant.12.clone.1), window={size=1x1x128 pad=0_0x0_0x127_0}, to_apply=%region_7.8 | reduce-window | flops 8323072 | bytes 524292 | tf_op jit(solution)/shard_map/reduce-window
  28.7 0.1 slice.12
  28.8 0.1 copy.37
  29.0 0.1 copy.38
  29.1 0.1 broadcast_add_fusion
  29.2 0.1 copy.32
  29.4 0.2 mul.109
  29.6 0.1 copy.39
  29.7 0.2 reshape.261
  29.9 0.1 fusion.25
  30.0 4.3 %scatter_custom_fusion = s32[2048]{0:T(1024)S(1)} fusion(s32[1024]{0:T(1024)S(1)} %bitcast.56, s32[1024]{0:T(1024)S(1)} %reshape.261, s32[]{:T(128)} %constant.12.clone.1), kind=kCustom, calls=%fused_computation.61 | custom fusion | bytes 8196 | tf_op jit(solution)/shard_map/scatter | solution.py:60
  34.3 0.7 all_to_all.14
  35.0 13.1 %all-to-all-start = ((s32[64,1,32]{2,1,0:T(1,128)}), s32[64,1,32]{2,1,0:T(1,128)S(1)}, u32[]{:S(2)}, u32[]{:S(2)}) async-start(s32[64,1,32]{2,1,0:T(1,128)} %bitcast.5), calls=%async_computation | async-start | bytes 65536 | tf_op jit(solution)/shard_map/all_to_all | solution.py:63
  48.2 0.6 fusion.10
  48.8 9.0 %all-reduce.1 = (f32[512]{0:T(512)S(1)}, f32[512]{0:T(512)S(1)}) all-reduce(f32[512]{0:T(512)S(1)} %get-tuple-element.8, f32[512]{0:T(512)S(1)} %get-tuple-element.7), channel_id=1, replica_groups=mesh['dp'=64,'section'=4] {'section'}, use_global_device_ids=true, to_apply=%region_3.0 | all-reduce | flops 1024 | bytes 8192 | tf_op jit(solution)/shard_map/psum | solution.py:38
  57.8 1.8 fusion.33
  59.6 0.1 reshape.243
  59.7 9.7 %gather_fusion = bf16[2048,1024]{1,0:T(8,128)(2,1)} fusion(bf16[512,1024]{1,0:T(8,128)(2,1)S(1)} %get-tuple-element.23, s32[2048]{0:T(1024)S(1)} %broadcast_clamp_fusion), kind=kCustom, calls=%fused_computation | custom fusion | bytes 8396800 | tf_op jit(solution)/shard_map/gather | solution.py:64
  69.4 12.0 %all-to-all-start.1 = ((bf16[64,32,1024]{2,1,0:T(8,128)(2,1)}), bf16[64,32,1024]{2,1,0:T(8,128)(2,1)}, u32[]{:S(2)}, u32[]{:S(2)}) async-start(bf16[64,32,1024]{2,1,0:T(8,128)(2,1)} %bitcast.46), calls=%async_computation.1 | async-start | bytes 8388608 | tf_op jit(solution)/shard_map/all_to_all | solution.py:65
  81.4 0.2 all-reduce.4.cloned.1.call-start
  81.6 2.8 convolution_convert_fusion
  84.4 0.0 all-reduce.4.cloned.1.call-update
  84.4 4.3 %broadcast_in_dim.32 = f32[512,2,1024]{2,1,0:T(2,128)} broadcast(bf16[512,1024]{1,0:T(8,128)(2,1)} %get-tuple-element.22), dimensions={0,2} | broadcast | bytes 5242880 | tf_op jit(solution)/shard_map/broadcast_in_dim | solution.py:88
  88.7 6.0 %convert_element_type.86 = f32[1024,1024]{1,0:T(8,128)} reshape(f32[512,2,1024]{2,1,0:T(2,128)} %broadcast_in_dim.32) | data formatting | bytes 8388608 | tf_op jit(solution)/shard_map/convert_element_type | solution.py:89
  94.7 35.9 %all-reduce.4.cloned.1.call-done = bf16[512,512]{1,0:T(8,128)(2,1)} async-done(((bf16[512,512]{1,0:T(8,128)(2,1)}), bf16[512,512]{1,0:T(8,128)(2,1)}) %all-reduce.4.cloned.1.call-update) | async-done | bytes 524304 | tf_op jit(solution)/shard_map/psum | solution.py:75
  130.7 1.5 fusion.18
  132.2 43.9 %all-to-all-done.1 = bf16[64,32,1024]{2,1,0:T(8,128)(2,1)} async-done(((bf16[64,32,1024]{2,1,0:T(8,128)(2,1)}), bf16[64,32,1024]{2,1,0:T(8,128)(2,1)}, u32[]{:S(2)}, u32[]{:S(2)}) %all-to-all-start.1) | async-done | bytes 4194336 | tf_op jit(solution)/shard_map/all_to_all | solution.py:65
  176.1 8.8 %gather_fusion.1 = bf16[1024,1024]{1,0:T(8,128)(2,1)} fusion(bf16[2048,1024]{1,0:T(8,128)(2,1)} %bitcast.8, s32[1024]{0:T(1024)S(1)} %broadcast_clamp_fusion.1), kind=kCustom, calls=%fused_computation.1 | custom fusion | bytes 4198400 | tf_op jit(solution)/shard_map/gather | solution.py:67
  184.9 4.1 reshape.234
  189.0 6.3 %fusion.14 = bf16[512,1,2]{2,1,0:T(2,128)(2,1)S(1)} fusion(bf16[512,2,1024]{2,1,0:T(2,128)(2,1)} %reshape.234, bf16[512,1024,1]{1,0,2:T(8,128)(2,1)} %bitcast.47), kind=kOutput, calls=%fused_computation.30 | convolution fusion | flops 2097152 | bytes 3147776 | tf_op jit(solution)/shard_map/qd,qkd->qk/dot_general | solution.py:73
  195.3 0.1 copy.43
  195.5 6.0 %psum.45 = bf16[512,2]{0,1:T(2,128)(2,1)S(1)} all-reduce(bf16[512,2]{0,1:T(2,128)(2,1)S(1)} %bitcast.54), channel_id=1, replica_groups=mesh['dp'=64,'section'=4] {'section'}, use_global_device_ids=true, to_apply=%region_11.12 | all-reduce | flops 1024 | bytes 4096 | tf_op jit(solution)/shard_map/psum | solution.py:76
  201.5 0.2 copy.41
  201.7 0.2 reshape.238
  201.9 10.1 %scatter_custom_fusion.1 = f32[2048,1024]{1,0:T(8,128)} fusion(s32[1024]{0:T(1024)S(1)} %bitcast.57, f32[1024,1024]{1,0:T(8,128)} %convert_element_type.86, f32[]{:T(128)} %constant.9.clone.1, f32[1024]{0:T(1024)S(1)} %reshape.238), kind=kCustom, calls=%fused_computation.7 | custom fusion | flops 1048576 | bytes 12587012 | tf_op jit(solution)/shard_map/scatter | solution.py:95
  212.0 6.0 %convert_element_type.87 = bf16[2048,1024]{1,0:T(8,128)(2,1)} convert(f32[2048,1024]{1,0:T(8,128)} %scatter_custom_fusion.1) | non-fusion elementwise | flops 2097152 | bytes 12582912 | tf_op jit(solution)/shard_map/convert_element_type | solution.py:98
  218.0 8.8 %all-to-all-start.2 = ((bf16[64,32,1024]{2,1,0:T(8,128)(2,1)}), bf16[64,32,1024]{2,1,0:T(8,128)(2,1)}, u32[]{:S(2)}, u32[]{:S(2)}) async-start(bf16[64,32,1024]{2,1,0:T(8,128)(2,1)} %bitcast.45), calls=%async_computation.2 | async-start | bytes 8388608 | tf_op jit(solution)/shard_map/all_to_all | solution.py:97
  226.8 0.5 broadcast.204
  227.4 0.7 reduce.3
  228.1 0.1 reshape.235
  228.2 0.2 copy.44
  228.4 3.8 fusion.34
  232.2 3.6 fusion.37
  235.9 85.9 %all-to-all-done.2 = bf16[64,32,1024]{2,1,0:T(8,128)(2,1)} async-done(((bf16[64,32,1024]{2,1,0:T(8,128)(2,1)}), bf16[64,32,1024]{2,1,0:T(8,128)(2,1)}, u32[]{:S(2)}, u32[]{:S(2)}) %all-to-all-start.2) | async-done | bytes 4194336 | tf_op jit(solution)/shard_map/all_to_all | solution.py:97
  321.7 21.0 %scatter_custom_fusion.2 = f32[512,1024]{1,0:T(8,128)} fusion(f32[512,1024]{1,0:T(8,128)} %fusion.34, s32[2048]{0:T(1024)S(1)} %bitcast.55, bf16[2048,1024]{1,0:T(8,128)(2,1)} %bitcast.16), kind=kCustom, calls=%fused_computation.5 | custom fusion | flops 4194304 | bytes 6291456 | tf_op jit(solution)/shard_map/scatter-add | solution.py:104
  342.7 5.2 %multiply_reduce_fusion = (f32[512]{0:T(512)S(1)}, f32[512]{0:T(512)S(1)}, f32[512,1024]{1,0:T(8,128)}) fusion(f32[512,1024]{1,0:T(8,128)} %scatter_custom_fusion.2, f32[512]{0:T(512)S(1)} %get-tuple-element.25, f32[1024]{0:T(1024)S(1)} %copy-done.4, bf16[512,1024]{1,0:T(8,128)(2,1)S(1)} %copy-done.1, f32[512]{0:T(512)S(1)} %get-tuple-element.26, ...), kind=kOutput, calls=%fused_computation.25 | convolution fusion | flops 544734208 | bytes 9979904 | tf_op jit(solution)/shard_map/dot_general | solution.py:81
  347.9 7.7 %all-reduce = (f32[512]{0:T(512)S(1)}, f32[512]{0:T(512)S(1)}) all-reduce(f32[512]{0:T(512)S(1)} %get-tuple-element.6, f32[512]{0:T(512)S(1)} %get-tuple-element.5), channel_id=1, replica_groups=mesh['dp'=64,'section'=4] {'section'}, use_global_device_ids=true, to_apply=%region_14.15 | all-reduce | flops 1024 | bytes 8192 | tf_op jit(solution)/shard_map/psum | solution.py:105
  355.6 2.4 fusion.12
  358.0 2.3 fusion.11
  360.3 47.4 %all-gather = f32[65536]{0:T(1024)S(1)} all-gather(f32[1024]{0:T(1024)S(1)} %add.127), channel_id=2, replica_groups=mesh['dp'=64,'section'=4] {'dp'}, dimensions={0}, use_global_device_ids=true | all-gather | bytes 266240 | tf_op jit(solution)/shard_map/all_gather | solution.py:116
  407.8 0.6 reduce_sum.112
  408.4 2.8 multiply_convert_fusion.1
  (28 shorter events, 0.3 us)
Async XLA Ops:
  7.2 22.4 %copy-start.6 = (s32[512,2]{0,1:T(2,128)S(1)}, s32[512,2]{0,1:T(2,128)}, u32[]{:S(2)}) copy-start(s32[512,2]{0,1:T(2,128)} %param.12) | copy-start | bytes 12292
  9.3 38.9 %copy-start = (bf16[512,1024]{1,0:T(8,128)(2,1)S(1)}, bf16[512,1024]{1,0:T(8,128)(2,1)}, u32[]{:S(2)}) copy-start(bf16[512,1024]{1,0:T(8,128)(2,1)} %param.7) | copy-start | bytes 3145732
  9.3 38.9 %copy-start.1 = (bf16[512,1024]{1,0:T(8,128)(2,1)S(1)}, bf16[512,1024]{1,0:T(8,128)(2,1)}, u32[]{:S(2)}) copy-start(bf16[512,1024]{1,0:T(8,128)(2,1)} %param.8) | copy-start | bytes 3145732
  9.3 38.9 %copy-start.4 = (f32[1024]{0:T(1024)S(1)}, f32[1024]{0:T(1024)}, u32[]{:S(2)}) copy-start(f32[1024]{0:T(1024)} %param.9) | copy-start | bytes 12292
  35.0 24.6 %all-to-all-start = ((s32[64,1,32]{2,1,0:T(1,128)}), s32[64,1,32]{2,1,0:T(1,128)S(1)}, u32[]{:S(2)}, u32[]{:S(2)}) async-start(s32[64,1,32]{2,1,0:T(1,128)} %bitcast.5), calls=%async_computation | async-start | bytes 65536 | tf_op jit(solution)/shard_map/all_to_all | solution.py:63
  69.4 106.7 %all-to-all-start.1 = ((bf16[64,32,1024]{2,1,0:T(8,128)(2,1)}), bf16[64,32,1024]{2,1,0:T(8,128)(2,1)}, u32[]{:S(2)}, u32[]{:S(2)}) async-start(bf16[64,32,1024]{2,1,0:T(8,128)(2,1)} %bitcast.46), calls=%async_computation.1 | async-start | bytes 8388608 | tf_op jit(solution)/shard_map/all_to_all | solution.py:65
  81.4 49.3 %all-reduce.4.cloned.1.call-start = ((), (), s32[]{:S(2)}) async-start(), calls=%async_computation.3 | async-start | bytes 1048576 | tf_op jit(solution)/shard_map/psum | solution.py:75
  88.7 42.0 %copy-start.7 = (s32[512]{0:T(512)S(1)}, s32[512]{0:T(512)}, u32[]{:S(2)}) copy-start(s32[512]{0:T(512)} %param.10) | copy-start | bytes 6148
  189.0 12.5 %copy-start.5 = (s32[512,2]{0,1:T(2,128)S(1)}, s32[512,2]{0,1:T(2,128)}, u32[]{:S(2)}) copy-start(s32[512,2]{0,1:T(2,128)} %param.13) | copy-start | bytes 12292
  218.0 103.7 %all-to-all-start.2 = ((bf16[64,32,1024]{2,1,0:T(8,128)(2,1)}), bf16[64,32,1024]{2,1,0:T(8,128)(2,1)}, u32[]{:S(2)}, u32[]{:S(2)}) async-start(bf16[64,32,1024]{2,1,0:T(8,128)(2,1)} %bitcast.45), calls=%async_computation.2 | async-start | bytes 8388608 | tf_op jit(solution)/shard_map/all_to_all | solution.py:97
  228.4 3.8 copy-start.3
  355.6 2.4 copy-start.2
Sparse Core Ops, SparseCore 0:
  85.1 45.5 all-reduce.3
